TPU v7x, 128 devices: a whole 4x4x4 slice. The times are simulated.
128 devices in a mesh: space: 8 (over x, core), win: 16 (over z, y).
Axes of the slice: x: 4, y: 4, z: 4, core: 2. Of those that a mesh axis runs over, the one named last changes fastest.
Arguments:
- snapshots: bfloat16 [128, 24576, 256], P('win', 'space'), as said below
- modes: bfloat16 [128, 24576, 256], P('win', 'space'), may hold values from -0.5 to 0.5
- amp_re: float32 [128, 128], P('win'), may hold values from -5 to 5
- amp_im: float32 [128, 128], P('win'), may hold values from -5 to 5
- growth: float32 [128, 128], P('win'), may hold values from -0.01171875 to 0.001953125
- freq: float32 [128, 128], P('win'), may hold values from -3.140625 to 3.140625
- mode_count: int32 [128], P('win'), may hold values from 8 to 128
- slot_window: int32 [128], P('win'), may hold values from 0 to 127, as said below
Outputs:
- gram: float32 [128, 256, 256], P('win')
Inputs may be any that keep to these rules, and one draw needn't show every extreme that they name: slot_window is a permutation of the 128 windows; slot j holds a window of the same position in its block, slot_window[j] % 8 == j % 8; the 8 slots of one block hold windows of 8 different blocks. Each point's snapshots share one scale.
All inputs are finite; a program needn't handle non-finite values.
Results may differ from a plain program's by a relative error of at most 0.0026.
Values may be sent and summed in bfloat16 or wider, within the bound.
A program may use at most 192 MiB of HBM per device.

v0:
```python
import jax
import jax.numpy as jnp
from jax import lax
from jax.sharding import PartitionSpec as P

K = 128
S = 256
WIN_DEV = 8


def coefficients(amp_re, amp_im, growth, freq, mode_count):
    steps = jnp.arange(S).astype(jnp.float32)
    live = (jnp.arange(K, dtype=jnp.int32)[None, :] < mode_count[:, None]).astype(jnp.float32)
    decay = jnp.exp(growth[:, :, None] * steps) * live[:, :, None]
    angle = freq[:, :, None] * steps
    cosine = jnp.cos(angle)
    sine = jnp.sin(angle)
    real_part = (amp_re[:, :, None] * cosine - amp_im[:, :, None] * sine) * decay
    imag_part = (amp_re[:, :, None] * sine + amp_im[:, :, None] * cosine) * decay
    stacked = jnp.stack([real_part, -imag_part], axis=2)
    return stacked.reshape(amp_re.shape[0], 2 * K, S).astype(jnp.bfloat16)


def batch_grams(slabs, vectors, coef):
    recon = jnp.einsum("wpk,wks->wps", vectors, coef, preferred_element_type=jnp.float32)
    resid = (slabs.astype(jnp.float32) - recon).astype(jnp.bfloat16)
    return jnp.einsum("wps,wpt->wst", resid, resid, preferred_element_type=jnp.float32)


def on_device(snapshots, modes, amp_re, amp_im, growth, freq, mode_count, slot_window):
    nblocks = lax.axis_size("win")
    points_all = snapshots.shape[1] * lax.axis_size("space")
    coef = coefficients(amp_re, amp_im, growth, freq, mode_count)
    dest = slot_window // WIN_DEV
    place = slot_window % WIN_DEV
    vec_buf = jnp.zeros((nblocks,) + modes.shape[1:], jnp.bfloat16).at[dest].set(modes)
    coef_buf = jnp.zeros((nblocks, 2 * K, S), jnp.bfloat16).at[dest].set(coef)
    mark_buf = (
        jnp.zeros((nblocks, 128), jnp.bfloat16)
        .at[dest, place]
        .set(jnp.ones((WIN_DEV,), jnp.bfloat16))
    )
    got_vec, got_coef, got_mark = (
        lax.all_to_all(vec_buf, "win", split_axis=0, concat_axis=0, tiled=True),
        lax.all_to_all(coef_buf, "win", split_axis=0, concat_axis=0, tiled=True),
        lax.all_to_all(mark_buf, "win", split_axis=0, concat_axis=0, tiled=True),
    )
    marks = got_mark[:, :WIN_DEV].astype(jnp.int32)
    source = jnp.sum(jnp.arange(nblocks, dtype=jnp.int32)[:, None] * marks, axis=0)
    partial_value = batch_grams(snapshots, got_vec[source], got_coef[source])
    total = lax.psum(partial_value, "space")
    return total / points_all


def solution(mesh):
    return jax.shard_map(
        on_device,
        mesh=mesh,
        in_specs=(
            P("win", "space", None),
            P("win", "space", None),
            P("win", None),
            P("win", None),
            P("win", None),
            P("win", None),
            P("win"),
            P("win"),
        ),
        out_specs=P("win", None, None),
        check_vma=False,
    )
```

profile of v0, /device:TPU:0, one launch (start us, length us, event | category | flops | bytes accessed | tf_op | source)
XLA Modules:
  0.0 555.7 jit_solution(11417734754348130964)
XLA Ops:
  6.5 0.7 fusion.18
  7.2 0.9 scatter_fusion.1
  8.1 0.6 copy.20
  8.7 8.2 %all-to-all-start.1 = ((bf16[16,1,128]{2,1,0:T(2,128)(2,1)}), bf16[16,1,128]{2,1,0:T(2,128)(2,1)S(1)}, u32[]{:S(2)}, u32[]{:S(2)}) async-start(bf16[16,1,128]{2,1,0:T(2,128)(2,1)} %copy.20), calls=%async_computation.1 | async-start | bytes 16384 | tf_op jit(solution)/shard_map/all_to_all | solution.py:46
  16.9 0.7 fusion.14
  17.6 5.3 fusion.9
  22.9 0.1 pad_maximum_fusion
  23.1 0.6 copy.21
  23.6 0.2 copy.22
  23.9 1.5 broadcast_in_dim.14
  25.4 2.8 scatter_fusion.2
  28.2 0.0 all-to-all-done.1
  28.2 7.2 %all-to-all-start.2 = ((bf16[16,256,256]{2,1,0:T(8,128)(2,1)}), bf16[16,256,256]{2,1,0:T(8,128)(2,1)S(1)}, u32[]{:S(2)}, u32[]{:S(2)}) async-start(bf16[16,256,256]{2,1,0:T(8,128)(2,1)} %scatter_fusion.2), calls=%async_computation.2 | async-start | bytes 4194304 | tf_op jit(solution)/shard_map/all_to_all | solution.py:45
  35.5 8.3 %broadcast_in_dim.10 = bf16[16,3072,256]{2,1,0:T(8,128)(2,1)} broadcast(bf16[]{:T(256)} %constant.32.clone.1), dimensions={} | broadcast | bytes 25165826 | tf_op jit(solution)/shard_map/broadcast_in_dim | solution.py:36
  43.8 25.7 %scatter_fusion = bf16[16,3072,256]{2,1,0:T(8,128)(2,1)} fusion(bf16[16,3072,256]{2,1,0:T(8,128)(2,1)} %broadcast_in_dim.10, s32[8]{0:T(128)S(1)} %get-tuple-element.6, bf16[8,3072,256]{2,1,0:T(8,128)(2,1)} %param.9), kind=kCustom, calls=%fused_computation.2 | custom fusion | bytes 37748768 | tf_op jit(solution)/shard_map/scatter | solution.py:36
  69.5 0.0 all-to-all-done.2
  69.5 7.4 %all-to-all-start = ((bf16[16,3072,256]{2,1,0:T(8,128)(2,1)}), bf16[16,3072,256]{2,1,0:T(8,128)(2,1)}, u32[]{:S(2)}, u32[]{:S(2)}) async-start(bf16[16,3072,256]{2,1,0:T(8,128)(2,1)} %scatter_fusion), calls=%async_computation | async-start | bytes 50331648 | tf_op jit(solution)/shard_map/all_to_all | solution.py:44
  76.9 0.0 all-reduce.2.cloned.1.call-start
  77.0 0.6 gather_fusion.1
  77.6 369.2 %all-to-all-done = bf16[16,3072,256]{2,1,0:T(8,128)(2,1)} async-done(((bf16[16,3072,256]{2,1,0:T(8,128)(2,1)}), bf16[16,3072,256]{2,1,0:T(8,128)(2,1)}, u32[]{:S(2)}, u32[]{:S(2)}) %all-to-all-start) | async-done | bytes 25165856 | tf_op jit(solution)/shard_map/all_to_all | solution.py:44
  446.8 14.6 %gather_fusion = bf16[8,3072,256]{2,1,0:T(8,128)(2,1)} fusion(bf16[16,3072,256]{2,1,0:T(8,128)(2,1)} %all-to-all-done, s32[1024]{0:T(1024)S(1)} %pad_clamp_fusion), kind=kCustom, calls=%fused_computation | custom fusion | bytes 25165856 | tf_op jit(solution)/shard_map/gather | solution.py:50
  461.4 19.9 %fusion = f32[8,256,256]{2,1,0:T(8,128)} fusion(bf16[8,3072,256]{2,1,0:T(8,128)(2,1)} %param.8, bf16[8,3072,256]{2,1,0:T(8,128)(2,1)} %gather_fusion, bf16[8,256,256]{2,1,0:T(8,128)(2,1)S(1)} %gather_fusion.1), kind=kOutput, calls=%fused_computation.6 | convolution fusion | flops 6461325312 | bytes 28311552 | tf_op jit(solution)/shard_map/wps,wpt->wst/dot_general | solution.py:27
  481.3 0.0 all-reduce.2.cloned.1.call-update
  481.4 64.4 %all-reduce.2.cloned.1.call-done = f32[8,256,256]{2,1,0:T(8,128)} async-done(((f32[8,256,256]{2,1,0:T(8,128)}), f32[8,256,256]{2,1,0:T(8,128)}) %all-reduce.2.cloned.1.call-update) | async-done | bytes 2097168 | tf_op jit(solution)/shard_map/psum | solution.py:51
  545.8 3.1 broadcast_multiply_fusion
  (7 shorter events, 0.1 us)
Async XLA Ops:
  8.7 19.5 %all-to-all-start.1 = ((bf16[16,1,128]{2,1,0:T(2,128)(2,1)}), bf16[16,1,128]{2,1,0:T(2,128)(2,1)S(1)}, u32[]{:S(2)}, u32[]{:S(2)}) async-start(bf16[16,1,128]{2,1,0:T(2,128)(2,1)} %copy.20), calls=%async_computation.1 | async-start | bytes 16384 | tf_op jit(solution)/shard_map/all_to_all | solution.py:46
  28.2 41.2 %all-to-all-start.2 = ((bf16[16,256,256]{2,1,0:T(8,128)(2,1)}), bf16[16,256,256]{2,1,0:T(8,128)(2,1)S(1)}, u32[]{:S(2)}, u32[]{:S(2)}) async-start(bf16[16,256,256]{2,1,0:T(8,128)(2,1)} %scatter_fusion.2), calls=%async_computation.2 | async-start | bytes 4194304 | tf_op jit(solution)/shard_map/all_to_all | solution.py:45
  69.5 377.3 %all-to-all-start = ((bf16[16,3072,256]{2,1,0:T(8,128)(2,1)}), bf16[16,3072,256]{2,1,0:T(8,128)(2,1)}, u32[]{:S(2)}, u32[]{:S(2)}) async-start(bf16[16,3072,256]{2,1,0:T(8,128)(2,1)} %scatter_fusion), calls=%async_computation | async-start | bytes 50331648 | tf_op jit(solution)/shard_map/all_to_all | solution.py:44
  76.9 468.9 %all-reduce.2.cloned.1.call-start = ((), (), s32[]{:S(2)}) async-start(), calls=%async_computation.3 | async-start | bytes 4194304 | tf_op jit(solution)/shard_map/psum | solution.py:51
Sparse Core Ops, SparseCore 0:
  481.5 64.2 all-reduce.1
where the time goes:
time: 556 us
  waiting for transfers between devices  434 us (78%)
  local copies, waits for them, and re-layouts  55.9 us (10%)
  starting transfers between devices  22.8 us (4%)
  matrix products  19.9 us (4%)
  between operations  13.5 us (2%)
  other arithmetic  9.96 us (2%)
    all_to_all x1, waiting for transfers between devices, on_device(): lax.all_to_all(vec_buf, 'win', split_axis=0, concat_axis=0, tiled=True)  369 us
    psum x1, waiting for transfers between devices, on_device(): total = lax.psum(partial_value, 'space')  64.4 us
    scatter x1, local copies, waits for them, and re-layouts, on_device(): jnp.zeros((nblocks,) + modes.shape[1:], jnp.bfloat16).at[dest].set(modes)  25.7 us
    dot_general x1, matrix products, batch_grams(): jnp.einsum('wps,wpt->wst', resid, resid, preferred_element_type=jnp.float32)  19.9 us
    gather x2, local copies, waits for them, and re-layouts, on_device(): partial_value = batch_grams(snapshots, got_vec[source], got_coef[source])  15.2 us
  transfers between devices with their start and end apart: 4, of which 2 were waited for; matrix products, arithmetic and copies ran while one was open for 8% of the time, Pallas kernels for 0%

commit v1 on v0

--- a/solution.py
+++ b/solution.py
@@ -6,6 +6,22 @@
 K = 128
 S = 256
 WIN_DEV = 8
+
+
+def pairwise_exchange(x, axis, split, join):
+    ways, here = (lax.axis_size(axis), lax.axis_index(axis))
+    width = x.shape[split] // ways
+    dims = list(x.shape)
+    dims[split] = width
+    height = dims[join]
+    dims[join] = height * ways
+    full = jnp.zeros(dims, x.dtype)
+    for mask in range(ways):
+        part = lax.dynamic_slice_in_dim(x, (here ^ mask) * width, width, axis=split)
+        if mask:
+            part = lax.ppermute(part, axis, [(d, d ^ mask) for d in range(ways)])
+        full = lax.dynamic_update_slice_in_dim(full, part, (here ^ mask) * height, axis=join)
+    return full
 
 
 def coefficients(amp_re, amp_im, growth, freq, mode_count):
@@ -41,7 +57,7 @@
         .set(jnp.ones((WIN_DEV,), jnp.bfloat16))
     )
     got_vec, got_coef, got_mark = (
-        lax.all_to_all(vec_buf, "win", split_axis=0, concat_axis=0, tiled=True),
+        pairwise_exchange(vec_buf, "win", 0, 0),
         lax.all_to_all(coef_buf, "win", split_axis=0, concat_axis=0, tiled=True),
         lax.all_to_all(mark_buf, "win", split_axis=0, concat_axis=0, tiled=True),
     )

time: 556 us -> 659 us (1.19)
  local copies, waits for them, and re-layouts: 55.9 us -> 108 us
  waiting for transfers between devices: 434 us -> 463 us
  starting transfers between devices: 22.8 us -> 45.6 us
    all_to_all x1 -> x0, waiting for transfers between devices: 369 us -> none  [on_device(): lax.all_to_all(vec_buf, 'win', split_axis=0, concat_axis=0, tiled=True)]
    ppermute x0 -> x15, waiting for transfers between devices: none -> 315 us  [pairwise_exchange(): part = lax.ppermute(part, axis, [(d, d ^ mask) for d in range(ways)])]
    all_to_all x1, waiting for transfers between devices: 0.01 us -> 82.9 us  [on_device(): lax.all_to_all(mark_buf, 'win', split_axis=0, concat_axis=0, tiled=True)]
    ppermute x0 -> x15, starting transfers between devices: none -> 33 us  [pairwise_exchange(): part = lax.ppermute(part, axis, [(d, d ^ mask) for d in range(ways)])]
    dynamic_update_slice x0 -> x15, local copies, waits for them, and re-layouts: none -> 26.2 us  [pairwise_exchange(): lax.dynamic_update_slice_in_dim(full, part, (here ^ mask) * height, axis=...]
    dynamic_slice x0 -> x1, local copies, waits for them, and re-layouts: none -> 17.2 us  [pairwise_exchange(): part = lax.dynamic_slice_in_dim(x, (here ^ mask) * width, width, axis=split)]
    another operation x1 -> x3, local copies, waits for them, and re-layouts: 0.01 us -> 16.9 us
    broadcast_in_dim x1 -> x0, local copies, waits for them, and re-layouts: 8.34 us -> none  [on_device(): jnp.zeros((nblocks,) + modes.shape[1:], jnp.bfloat16).at[dest].set(modes)]
  transfers between devices with their start and end apart: 4 -> 18, of which waited for: 2 -> 6; matrix products, arithmetic and copies ran while one was open for 8% -> 8% of each run, Pallas kernels for 0% -> 0%
where the time goes in v1:
time: 659 us
  waiting for transfers between devices  463 us (70%)
  local copies, waits for them, and re-layouts  108 us (16%)
  starting transfers between devices  45.6 us (7%)
  matrix products  19.9 us (3%)
  between operations  13.7 us (2%)
  other arithmetic  8.51 us (1%)
    ppermute x15, waiting for transfers between devices, pairwise_exchange(): part = lax.ppermute(part, axis, [(d, d ^ mask) for d in range(ways)])  315 us
    all_to_all x1, waiting for transfers between devices, on_device(): lax.all_to_all(mark_buf, 'win', split_axis=0, concat_axis=0, tiled=True)  82.9 us
    psum x1, waiting for transfers between devices, on_device(): total = lax.psum(partial_value, 'space')  65 us
    ppermute x15, starting transfers between devices, pairwise_exchange(): part = lax.ppermute(part, axis, [(d, d ^ mask) for d in range(ways)])  33 us
    dynamic_update_slice x15, local copies, waits for them, and re-layouts, pairwise_exchange(): lax.dynamic_update_slice_in_dim(full, part, (here ^ mask) * height, axis=...  26.2 us
    scatter x1, local copies, waits for them, and re-layouts, on_device(): jnp.zeros((nblocks,) + modes.shape[1:], jnp.bfloat16).at[dest].set(modes)  25.7 us
    dot_general x1, matrix products, batch_grams(): jnp.einsum('wps,wpt->wst', resid, resid, preferred_element_type=jnp.float32)  19.9 us
    dynamic_slice x1, local copies, waits for them, and re-layouts, pairwise_exchange(): part = lax.dynamic_slice_in_dim(x, (here ^ mask) * width, width, axis=split)  17.2 us
  transfers between devices with their start and end apart: 18, of which 6 were waited for; matrix products, arithmetic and copies ran while one was open for 8% of the time, Pallas kernels for 0%

profile of v1, /device:TPU:0, one launch (start us, length us, event | category | flops | bytes accessed | tf_op | source)
XLA Modules:
  0.0 658.7 jit_solution(2392851222058918429)
XLA Ops:
  7.3 8.4 %broadcast.148.clone = bf16[16,3072,256]{2,1,0:T(8,128)(2,1)} broadcast(bf16[]{:T(256)} %constant.23.clone.1), dimensions={} | broadcast | bytes 25165826 | tf_op jit(solution)/shard_map/broadcast.15
  15.7 25.7 %scatter_fusion = bf16[16,3072,256]{2,1,0:T(8,128)(2,1)} fusion(bf16[16,3072,256]{2,1,0:T(8,128)(2,1)} %broadcast.148.clone, s32[8]{0:T(128)S(1)} %get-tuple-element.6, bf16[8,3072,256]{2,1,0:T(8,128)(2,1)} %param.9), kind=kCustom, calls=%fused_computation.2 | custom fusion | bytes 37748768 | tf_op jit(solution)/shard_map/scatter | solution.py:52
  41.4 8.4 %broadcast.148 = bf16[16,3072,256]{2,1,0:T(8,128)(2,1)} broadcast(bf16[]{:T(256)} %constant.23.clone.1), dimensions={} | broadcast | bytes 25165826 | tf_op jit(solution)/shard_map/broadcast.15
  49.9 17.2 %constant_dynamic-slice_fusion = (bf16[1,3072,256]{2,1,0:T(8,128)(2,1)}, bf16[1,3072,256]{2,1,0:T(8,128)(2,1)}, bf16[1,3072,256]{2,1,0:T(8,128)(2,1)}, bf16[1,30...) fusion(bf16[16,3072,256]{2,1,0:T(8,128)(2,1)} %scatter_fusion, ...), kind=kLoop, calls=%fused_computation.27 | loop fusion | bytes 50331712 | tf_op jit(solution)/shard_map/dynamic_slice | solution.py:20
  67.1 2.0 collective-permute-start
  69.0 2.7 collective-permute-start.1
  71.9 2.3 collective-permute-start.3
  75.7 8.8 %all-to-all-start = ((bf16[16,1,128]{2,1,0:T(2,128)(2,1)}), bf16[16,1,128]{2,1,0:T(2,128)(2,1)S(1)}, u32[]{:S(2)}, u32[]{:S(2)}) async-start(bf16[16,1,128]{2,1,0:T(2,128)(2,1)} %copy.20), calls=%async_computation | async-start | bytes 16384 | tf_op jit(solution)/shard_map/all_to_all | solution.py:62
  84.6 4.5 fusion.9
  90.1 1.5 broadcast_in_dim.11
  91.6 2.8 scatter_fusion.2
  94.4 82.9 %all-to-all-done = bf16[16,1,128]{2,1,0:T(2,128)(2,1)S(1)} async-done(((bf16[16,1,128]{2,1,0:T(2,128)(2,1)}), bf16[16,1,128]{2,1,0:T(2,128)(2,1)S(1)}, u32[]{:S(2)}, u32[]{:S(2)}) %all-to-all-start) | async-done | bytes 4128 | tf_op jit(solution)/shard_map/all_to_all | solution.py:62
  177.3 3.7 all-to-all-start.1
  181.2 4.3 collective-permute-start.5
  185.5 2.8 constant_dynamic-update-slice_fusion.14
  189.6 2.7 constant_dynamic-update-slice_fusion.13
  192.3 2.9 collective-permute-start.7
  195.1 2.7 constant_dynamic-update-slice_fusion.12
  197.8 2.6 constant_dynamic-update-slice_fusion.11
  200.5 6.0 collective-permute-start.9
  206.5 2.7 constant_dynamic-update-slice_fusion.10
  209.2 37.9 %collective-permute-done.5 = bf16[1,3072,256]{2,1,0:T(8,128)(2,1)S(1)} collective-permute-done((bf16[1,3072,256]{2,1,0:T(8,128)(2,1)}, bf16[1,3072,256]{2,1,0:T(8,128)(2,1)S(1)}, u32[]{:S(2)}, u32[]{:S(2)}) %collective-permute-start.5) | collective-permute-done | bytes 1572896 | tf_op jit(solution)/shard_map/ppermute | solution.py:22
  247.1 2.7 collective-permute-start.10
  251.0 50.2 %collective-permute-done.6 = bf16[1,3072,256]{2,1,0:T(8,128)(2,1)S(1)} collective-permute-done((bf16[1,3072,256]{2,1,0:T(8,128)(2,1)}, bf16[1,3072,256]{2,1,0:T(8,128)(2,1)S(1)}, u32[]{:S(2)}, u32[]{:S(2)}) %collective-permute-start.6) | collective-permute-done | bytes 1572896 | tf_op jit(solution)/shard_map/ppermute | solution.py:22
  303.9 104.8 %collective-permute-done.7 = bf16[1,3072,256]{2,1,0:T(8,128)(2,1)S(1)} collective-permute-done((bf16[1,3072,256]{2,1,0:T(8,128)(2,1)}, bf16[1,3072,256]{2,1,0:T(8,128)(2,1)S(1)}, u32[]{:S(2)}, u32[]{:S(2)}) %collective-permute-start.7) | collective-permute-done | bytes 1572896 | tf_op jit(solution)/shard_map/ppermute | solution.py:22
  408.7 2.1 collective-permute-start.12
  412.1 4.2 collective-permute-start.13
  421.2 122.3 %collective-permute-done.11 = bf16[1,3072,256]{2,1,0:T(8,128)(2,1)S(1)} collective-permute-done((bf16[1,3072,256]{2,1,0:T(8,128)(2,1)S(1)}, bf16[1,3072,256]{2,1,0:T(8,128)(2,1)S(1)}, u32[]{:S(2)}, u32[]{:S(2)}) %collective-permute-start.11) | collective-permute-done | bytes 1572896 | tf_op jit(solution)/shard_map/ppermute | solution.py:22
  548.6 14.6 %gather_fusion = bf16[8,3072,256]{2,1,0:T(8,128)(2,1)} fusion(bf16[16,3072,256]{2,1,0:T(8,128)(2,1)} %constant_dynamic-update-slice_fusion, s32[1024]{0:T(1024)S(1)} %pad_clamp_fusion), kind=kCustom, calls=%fused_computation | custom fusion | bytes 25165856 | tf_op jit(solution)/shard_map/gather | solution.py:66
  563.8 19.9 %fusion = f32[8,256,256]{2,1,0:T(8,128)} fusion(bf16[8,3072,256]{2,1,0:T(8,128)(2,1)} %param.8, bf16[8,3072,256]{2,1,0:T(8,128)(2,1)} %gather_fusion, bf16[8,256,256]{2,1,0:T(8,128)(2,1)S(1)} %gather_fusion.1), kind=kOutput, calls=%fused_computation.6 | convolution fusion | flops 6461325312 | bytes 28311552 | tf_op jit(solution)/shard_map/wps,wpt->wst/dot_general | solution.py:43
  583.8 65.0 %all-reduce.2.cloned.1.call-done = f32[8,256,256]{2,1,0:T(8,128)} async-done(((f32[8,256,256]{2,1,0:T(8,128)}), f32[8,256,256]{2,1,0:T(8,128)}) %all-reduce.2.cloned.1.call-update) | async-done | bytes 2097168 | tf_op jit(solution)/shard_map/psum | solution.py:67
  648.7 3.1 broadcast_multiply_fusion
  (67 shorter events, 20.6 us)
Async XLA Ops:
  49.8 34.7 %copy-start.6 = (s32[8]{0:T(128)S(1)}, s32[8]{0:T(128)}, u32[]{:S(2)}) copy-start(s32[8]{0:T(128)} %param.14) | copy-start | bytes 100
  49.8 34.7 %copy-start.7 = (f32[8,128]{1,0:T(8,128)S(1)}, f32[8,128]{1,0:T(8,128)}, u32[]{:S(2)}) copy-start(f32[8,128]{1,0:T(8,128)} %param.12) | copy-start | bytes 12292
  49.8 34.7 %copy-start.8 = (f32[8,128]{1,0:T(8,128)S(1)}, f32[8,128]{1,0:T(8,128)}, u32[]{:S(2)}) copy-start(f32[8,128]{1,0:T(8,128)} %param.11) | copy-start | bytes 12292
  49.8 34.8 %copy-start.9 = (f32[8,128]{1,0:T(8,128)S(1)}, f32[8,128]{1,0:T(8,128)}, u32[]{:S(2)}) copy-start(f32[8,128]{1,0:T(8,128)} %param.13) | copy-start | bytes 12292
  49.9 34.7 %copy-start.10 = (f32[8,128]{1,0:T(8,128)S(1)}, f32[8,128]{1,0:T(8,128)}, u32[]{:S(2)}) copy-start(f32[8,128]{1,0:T(8,128)} %param.10) | copy-start | bytes 12292
  67.1 114.1 %collective-permute-start = (bf16[1,3072,256]{2,1,0:T(8,128)(2,1)}, bf16[1,3072,256]{2,1,0:T(8,128)(2,1)}, u32[]{:S(2)}, u32[]{:S(2)}) collective-permute-start(bf16[1,3072,256]{2,1,0:T(8,128)(2,1)} %get-tuple-element.21), channel_id=1, source_target_pairs={{0,1},{1,0},{2,3},{3,2},{4,5},{5,4},{6,7},{7,6},{8,9},{9,8},{10,11... | collective-permute-start | bytes 4718600 | tf_op jit(solution)/shard_map/ppermute | solution.py:22
  69.0 119.3 %collective-permute-start.1 = (bf16[1,3072,256]{2,1,0:T(8,128)(2,1)}, bf16[1,3072,256]{2,1,0:T(8,128)(2,1)}, u32[]{:S(2)}, u32[]{:S(2)}) collective-permute-start(bf16[1,3072,256]{2,1,0:T(8,128)(2,1)} %get-tuple-element.20), channel_id=1, source_target_pairs={{0,2},{1,3},{2,0},{3,1},{4,6},{5,7},{6,4},{7,5},{8,10},{9,11},{10,... | collective-permute-start | bytes 4718600 | tf_op jit(solution)/shard_map/ppermute | solution.py:22
  71.8 120.5 %collective-permute-start.2 = (bf16[1,3072,256]{2,1,0:T(8,128)(2,1)}, bf16[1,3072,256]{2,1,0:T(8,128)(2,1)}, u32[]{:S(2)}, u32[]{:S(2)}) collective-permute-start(bf16[1,3072,256]{2,1,0:T(8,128)(2,1)} %get-tuple-element.19), channel_id=1, source_target_pairs={{0,3},{1,2},{2,1},{3,0},{4,7},{5,6},{6,5},{7,4},{8,11},{9,10},{10,... | collective-permute-start | bytes 4718600 | tf_op jit(solution)/shard_map/ppermute | solution.py:22
  71.9 126.0 %collective-permute-start.3 = (bf16[1,3072,256]{2,1,0:T(8,128)(2,1)}, bf16[1,3072,256]{2,1,0:T(8,128)(2,1)}, u32[]{:S(2)}, u32[]{:S(2)}) collective-permute-start(bf16[1,3072,256]{2,1,0:T(8,128)(2,1)} %get-tuple-element.18), channel_id=1, source_target_pairs={{0,4},{1,5},{2,6},{3,7},{4,0},{5,1},{6,2},{7,3},{8,12},{9,13},{10,... | collective-permute-start | bytes 4718600 | tf_op jit(solution)/shard_map/ppermute | solution.py:22
  74.2 126.3 %collective-permute-start.4 = (bf16[1,3072,256]{2,1,0:T(8,128)(2,1)}, bf16[1,3072,256]{2,1,0:T(8,128)(2,1)}, u32[]{:S(2)}, u32[]{:S(2)}) collective-permute-start(bf16[1,3072,256]{2,1,0:T(8,128)(2,1)} %get-tuple-element.17), channel_id=1, source_target_pairs={{0,5},{1,4},{2,7},{3,6},{4,1},{5,0},{6,3},{7,2},{8,13},{9,12},{10,... | collective-permute-start | bytes 4718600 | tf_op jit(solution)/shard_map/ppermute | solution.py:22
  75.7 101.7 %all-to-all-start = ((bf16[16,1,128]{2,1,0:T(2,128)(2,1)}), bf16[16,1,128]{2,1,0:T(2,128)(2,1)S(1)}, u32[]{:S(2)}, u32[]{:S(2)}) async-start(bf16[16,1,128]{2,1,0:T(2,128)(2,1)} %copy.20), calls=%async_computation | async-start | bytes 16384 | tf_op jit(solution)/shard_map/all_to_all | solution.py:62
  177.3 385.9 %all-to-all-start.1 = ((bf16[16,256,256]{2,1,0:T(8,128)(2,1)}), bf16[16,256,256]{2,1,0:T(8,128)(2,1)S(1)}, u32[]{:S(2)}, u32[]{:S(2)}) async-start(bf16[16,256,256]{2,1,0:T(8,128)(2,1)} %scatter_fusion.2), calls=%async_computation.1 | async-start | bytes 4194304 | tf_op jit(solution)/shard_map/all_to_all | solution.py:61
  181.1 467.7 %all-reduce.2.cloned.1.call-start = ((), (), s32[]{:S(2)}) async-start(), calls=%async_computation.2 | async-start | bytes 4194304 | tf_op jit(solution)/shard_map/psum | solution.py:67
  181.1 19.4 %copy-start.5 = (bf16[1,3072,256]{2,1,0:T(8,128)(2,1)S(1)}, bf16[1,3072,256]{2,1,0:T(8,128)(2,1)}, u32[]{:S(2)}) copy-start(bf16[1,3072,256]{2,1,0:T(8,128)(2,1)} %get-tuple-element.12) | copy-start | bytes 4718596
  181.1 66.0 %copy-start.4 = (bf16[1,3072,256]{2,1,0:T(8,128)(2,1)S(1)}, bf16[1,3072,256]{2,1,0:T(8,128)(2,1)}, u32[]{:S(2)}) copy-start(bf16[1,3072,256]{2,1,0:T(8,128)(2,1)} %get-tuple-element.11) | copy-start | bytes 4718596
  181.1 120.0 %copy-start.3 = (bf16[1,3072,256]{2,1,0:T(8,128)(2,1)S(1)}, bf16[1,3072,256]{2,1,0:T(8,128)(2,1)}, u32[]{:S(2)}) copy-start(bf16[1,3072,256]{2,1,0:T(8,128)(2,1)} %get-tuple-element.10) | copy-start | bytes 4718596
  181.1 227.6 %copy-start.2 = (bf16[1,3072,256]{2,1,0:T(8,128)(2,1)S(1)}, bf16[1,3072,256]{2,1,0:T(8,128)(2,1)}, u32[]{:S(2)}) copy-start(bf16[1,3072,256]{2,1,0:T(8,128)(2,1)} %get-tuple-element.9) | copy-start | bytes 4718596
  181.2 65.9 %collective-permute-start.5 = (bf16[1,3072,256]{2,1,0:T(8,128)(2,1)}, bf16[1,3072,256]{2,1,0:T(8,128)(2,1)S(1)}, u32[]{:S(2)}, u32[]{:S(2)}) collective-permute-start(bf16[1,3072,256]{2,1,0:T(8,128)(2,1)} %get-tuple-element.16), channel_id=1, source_target_pairs={{0,6},{1,7},{2,4},{3,5},{4,2},{5,3},{6,0},{7,1},{8,14},{9,15},{10,... | collective-permute-start | bytes 4718600 | tf_op jit(solution)/shard_map/ppermute | solution.py:22
  185.5 226.5 %copy-start.1 = (bf16[1,3072,256]{2,1,0:T(8,128)(2,1)S(1)}, bf16[1,3072,256]{2,1,0:T(8,128)(2,1)}, u32[]{:S(2)}) copy-start(bf16[1,3072,256]{2,1,0:T(8,128)(2,1)} %get-tuple-element.8) | copy-start | bytes 4718596
  188.3 229.2 %copy-start = (bf16[1,3072,256]{2,1,0:T(8,128)(2,1)S(1)}, bf16[1,3072,256]{2,1,0:T(8,128)(2,1)}, u32[]{:S(2)}) copy-start(bf16[1,3072,256]{2,1,0:T(8,128)(2,1)} %get-tuple-element.7) | copy-start | bytes 4718596
  188.3 112.8 %collective-permute-start.6 = (bf16[1,3072,256]{2,1,0:T(8,128)(2,1)}, bf16[1,3072,256]{2,1,0:T(8,128)(2,1)S(1)}, u32[]{:S(2)}, u32[]{:S(2)}) collective-permute-start(bf16[1,3072,256]{2,1,0:T(8,128)(2,1)} %get-tuple-element.15), channel_id=1, source_target_pairs={{0,7},{1,6},{2,5},{3,4},{4,3},{5,2},{6,1},{7,0},{8,15},{9,14},{10,... | collective-permute-start | bytes 4718600 | tf_op jit(solution)/shard_map/ppermute | solution.py:22
  192.3 216.4 %collective-permute-start.7 = (bf16[1,3072,256]{2,1,0:T(8,128)(2,1)}, bf16[1,3072,256]{2,1,0:T(8,128)(2,1)S(1)}, u32[]{:S(2)}, u32[]{:S(2)}) collective-permute-start(bf16[1,3072,256]{2,1,0:T(8,128)(2,1)} %get-tuple-element.14), channel_id=1, source_target_pairs={{0,8},{1,9},{2,10},{3,11},{4,12},{5,13},{6,14},{7,15},{8,0},{9,1},... | collective-permute-start | bytes 4718600 | tf_op jit(solution)/shard_map/ppermute | solution.py:22
  197.8 214.2 %collective-permute-start.8 = (bf16[1,3072,256]{2,1,0:T(8,128)(2,1)}, bf16[1,3072,256]{2,1,0:T(8,128)(2,1)S(1)}, u32[]{:S(2)}, u32[]{:S(2)}) collective-permute-start(bf16[1,3072,256]{2,1,0:T(8,128)(2,1)} %get-tuple-element.13), channel_id=1, source_target_pairs={{0,9},{1,8},{2,11},{3,10},{4,13},{5,12},{6,15},{7,14},{8,1},{9,0},... | collective-permute-start | bytes 4718600 | tf_op jit(solution)/shard_map/ppermute | solution.py:22
  200.5 217.0 %collective-permute-start.9 = (bf16[1,3072,256]{2,1,0:T(8,128)(2,1)S(1)}, bf16[1,3072,256]{2,1,0:T(8,128)(2,1)S(1)}, u32[]{:S(2)}, u32[]{:S(2)}) collective-permute-start(bf16[1,3072,256]{2,1,0:T(8,128)(2,1)S(1)} %copy-done.5), channel_id=1, source_target_pairs={{0,10},{1,11},{2,8},{3,9},{4,14},{5,15},{6,12},{7,13},{8,2},{9,3},... | collective-permute-start | bytes 4718600 | tf_op jit(solution)/shard_map/ppermute | solution.py:22
  247.1 172.8 %collective-permute-start.10 = (bf16[1,3072,256]{2,1,0:T(8,128)(2,1)S(1)}, bf16[1,3072,256]{2,1,0:T(8,128)(2,1)S(1)}, u32[]{:S(2)}, u32[]{:S(2)}) collective-permute-start(bf16[1,3072,256]{2,1,0:T(8,128)(2,1)S(1)} %copy-done.4), channel_id=1, source_target_pairs={{0,11},{1,10},{2,9},{3,8},{4,15},{5,14},{6,13},{7,12},{8,3},{9,2},... | collective-permute-start | bytes 4718600 | tf_op jit(solution)/shard_map/ppermute | solution.py:22
  301.1 242.3 %collective-permute-start.11 = (bf16[1,3072,256]{2,1,0:T(8,128)(2,1)S(1)}, bf16[1,3072,256]{2,1,0:T(8,128)(2,1)S(1)}, u32[]{:S(2)}, u32[]{:S(2)}) collective-permute-start(bf16[1,3072,256]{2,1,0:T(8,128)(2,1)S(1)} %copy-done.3), channel_id=1, source_target_pairs={{0,12},{1,13},{2,14},{3,15},{4,8},{5,9},{6,10},{7,11},{8,4},{9,5},... | collective-permute-start | bytes 4718600 | tf_op jit(solution)/shard_map/ppermute | solution.py:22
  408.7 136.0 %collective-permute-start.12 = (bf16[1,3072,256]{2,1,0:T(8,128)(2,1)S(1)}, bf16[1,3072,256]{2,1,0:T(8,128)(2,1)S(1)}, u32[]{:S(2)}, u32[]{:S(2)}) collective-permute-start(bf16[1,3072,256]{2,1,0:T(8,128)(2,1)S(1)} %copy-done.2), channel_id=1, source_target_pairs={{0,13},{1,12},{2,15},{3,14},{4,9},{5,8},{6,11},{7,10},{8,5},{9,4},... | collective-permute-start | bytes 4718600 | tf_op jit(solution)/shard_map/ppermute | solution.py:22
  412.1 133.9 %collective-permute-start.13 = (bf16[1,3072,256]{2,1,0:T(8,128)(2,1)S(1)}, bf16[1,3072,256]{2,1,0:T(8,128)(2,1)S(1)}, u32[]{:S(2)}, u32[]{:S(2)}) collective-permute-start(bf16[1,3072,256]{2,1,0:T(8,128)(2,1)S(1)} %copy-done.1), channel_id=1, source_target_pairs={{0,14},{1,15},{2,12},{3,13},{4,10},{5,11},{6,8},{7,9},{8,6},{9,7},... | collective-permute-start | bytes 4718600 | tf_op jit(solution)/shard_map/ppermute | solution.py:22
  417.5 129.8 %collective-permute-start.14 = (bf16[1,3072,256]{2,1,0:T(8,128)(2,1)S(1)}, bf16[1,3072,256]{2,1,0:T(8,128)(2,1)S(1)}, u32[]{:S(2)}, u32[]{:S(2)}) collective-permute-start(bf16[1,3072,256]{2,1,0:T(8,128)(2,1)S(1)} %copy-done), channel_id=1, source_target_pairs={{0,15},{1,14},{2,13},{3,12},{4,11},{5,10},{6,9},{7,8},{8,7},{9,6},... | collective-permute-start | bytes 4718600 | tf_op jit(solution)/shard_map/ppermute | solution.py:22
Sparse Core Ops, SparseCore 0:
  583.9 64.8 all-reduce.1
